TPU v7x, 32 devices: a whole 2x2x4 slice. The times are simulated.
32 devices in a mesh: dp: 16 (over z, y, core), mp: 2 (over x).
Axes of the slice: x: 2, y: 2, z: 4, core: 2. Of those that a mesh axis runs over, the one named last changes fastest.
Arguments:
- hidden_in: bfloat16 [32768, 1024], P(('dp', 'mp')), may hold values from -6 to 6
- out_grad: bfloat16 [32768, 1024], P(('dp', 'mp')), may hold values from -6 to 6
- ln1_gain: float32 [1024], replicated, may hold values from 0.5 to 1.5
- ln1_bias: float32 [1024], replicated, may hold values from -3 to 3
- w_query: bfloat16 [1024, 1024], P(None, 'mp'), may hold values from -0.1875 to 0.1875
- w_key: bfloat16 [1024, 1024], P(None, 'mp'), may hold values from -0.1875 to 0.1875
- w_value: bfloat16 [1024, 1024], P(None, 'mp'), may hold values from -0.1875 to 0.1875
- w_out: bfloat16 [1024, 1024], P('mp'), may hold values from -1.5 to 1.5
- ln2_gain: float32 [1024], replicated, may hold values from 0.5 to 1.5
- ln2_bias: float32 [1024], replicated, may hold values from -3 to 3
- w_up: bfloat16 [1024, 4096], P(None, 'mp'), may hold values from -0.1875 to 0.1875
- b_up: float32 [4096], P('mp'), may hold values from -3 to 3
- w_down: bfloat16 [4096, 1024], P('mp'), may hold values from -0.09375 to 0.09375
- b_down: float32 [1024], replicated, may hold values from -3 to 3
- rand_blocks: int32 [16, 16, 3], P('mp'), may hold values from 0 to 15
Outputs:
- output: bfloat16 [32768, 1024], P(('dp', 'mp'))
- input_grad: float32 [32768, 1024], P(('dp', 'mp'))
- grad_ln1_gain: float32 [1024], replicated
- grad_ln1_bias: float32 [1024], replicated
- grad_w_query: float32 [1024, 1024], P(None, 'mp')
- grad_w_key: float32 [1024, 1024], P(None, 'mp')
- grad_w_value: float32 [1024, 1024], P(None, 'mp')
- grad_w_out: float32 [1024, 1024], P('mp')
- grad_ln2_gain: float32 [1024], replicated
- grad_ln2_bias: float32 [1024], replicated
- grad_w_up: float32 [1024, 4096], P(None, 'mp')
- grad_b_up: float32 [4096], P('mp')
- grad_w_down: float32 [4096, 1024], P('mp')
- grad_b_down: float32 [1024], replicated
Inputs may be any that keep to these rules, and one draw needn't show every extreme that they name: rand_blocks[h, i, r] is a key block of the same sequence; entries may repeat or fall on window or global blocks, and those of the first and last query blocks have no effect.
All inputs are finite; a program needn't handle non-finite values.
Results may differ from a plain program's by a relative error of at most 0.02.
Values may be sent and summed in bfloat16 or wider, within the bound.
A program may use at most 320 MiB of HBM per device.

v0:
```python
import jax
import jax.numpy as jnp
from jax import lax
from jax.sharding import PartitionSpec as P

HD = 64
BLOCK = 64
SEQ = 1024


def layer_norm(values, norm_gain, norm_bias):
    center = values - jnp.mean(values, axis=-1, keepdims=True)
    spread = jnp.mean(center * center, axis=-1, keepdims=True)
    return center * lax.rsqrt(spread + 1e-05) * norm_gain + norm_bias


def block_mask(rand_blocks):
    blocks = SEQ // BLOCK
    row_ids = jnp.arange(blocks)[:, None]
    col_ids = jnp.arange(blocks)[None, :]
    window = (
        (jnp.abs(row_ids - col_ids) <= 1)
        | (col_ids == 0)
        | (col_ids == blocks - 1)
        | (row_ids == 0)
        | (row_ids == blocks - 1)
    )
    picked = jnp.any(rand_blocks[:, :, :, None] == jnp.arange(blocks)[None, None, None, :], axis=2)
    allowed = window[None] | picked
    return jnp.repeat(jnp.repeat(allowed, BLOCK, axis=1), BLOCK, axis=2)


def attend_forward(joined_seq, allowed, scaling):
    queries = joined_seq[:, 0]
    key_rows = joined_seq[:, 1]
    value_rows = joined_seq[:, 2]
    scores = (
        jnp.einsum("qhd,khd->hqk", queries, key_rows, preferred_element_type=jnp.float32) * scaling
    )
    scores = jnp.where(allowed, scores, -1e30)
    highest = jnp.max(scores, axis=-1, keepdims=True)
    shifted = jnp.exp(scores - highest)
    row_totals = jnp.sum(shifted, axis=-1, keepdims=True)
    attn_probs = (shifted / row_totals).astype(jnp.bfloat16)
    context = jnp.einsum("hqk,khd->qhd", attn_probs, value_rows, preferred_element_type=jnp.float32)
    return (context.astype(jnp.bfloat16), (highest + jnp.log(row_totals))[..., 0])


def attend_backward(seq_items, allowed, scaling):
    joined_seq, grad_context, row_lse = seq_items
    queries = joined_seq[:, 0]
    key_rows = joined_seq[:, 1]
    value_rows = joined_seq[:, 2]
    scores = (
        jnp.einsum("qhd,khd->hqk", queries, key_rows, preferred_element_type=jnp.float32) * scaling
    )
    scores = jnp.where(allowed, scores, -1e30)
    attn_probs = jnp.exp(scores - row_lse[..., None])
    grad_values = jnp.einsum(
        "hqk,qhd->khd",
        attn_probs.astype(jnp.bfloat16),
        grad_context,
        preferred_element_type=jnp.float32,
    ).astype(jnp.bfloat16)
    grad_probs = jnp.einsum(
        "qhd,khd->hqk", grad_context, value_rows, preferred_element_type=jnp.float32
    )
    row_inner = jnp.sum(grad_probs * attn_probs, axis=-1, keepdims=True)
    grad_scores = (attn_probs * (grad_probs - row_inner)).astype(jnp.bfloat16)
    grad_queries = (
        jnp.einsum("hqk,khd->qhd", grad_scores, key_rows, preferred_element_type=jnp.float32)
        * scaling
    ).astype(jnp.bfloat16)
    grad_keys = (
        jnp.einsum("hqk,qhd->khd", grad_scores, queries, preferred_element_type=jnp.float32)
        * scaling
    ).astype(jnp.bfloat16)
    return jnp.stack([grad_queries, grad_keys, grad_values], axis=1)


def per_device(
    hidden_in,
    out_grad,
    ln1_gain,
    ln1_bias,
    w_query,
    w_key,
    w_value,
    w_out,
    ln2_gain,
    ln2_bias,
    w_up,
    b_up,
    w_down,
    b_down,
    rand_blocks,
):
    local_heads = rand_blocks.shape[0]
    head_width = local_heads * HD
    local_rows = hidden_in.shape[0]
    seq_count = local_rows * lax.axis_size("mp") // SEQ
    scaling = HD ** (-0.5)
    allowed = block_mask(rand_blocks)
    inputs = hidden_in.astype(jnp.float32)
    w_joined = jnp.concatenate([w_query, w_key, w_value], axis=1)
    normed_one = layer_norm(inputs, ln1_gain, ln1_bias).astype(jnp.bfloat16)
    rows_one = lax.all_gather(normed_one, "mp", axis=0, tiled=True)
    joined = jnp.dot(rows_one, w_joined, preferred_element_type=jnp.float32).astype(jnp.bfloat16)
    joined_seq = joined.reshape(seq_count, SEQ, 3, local_heads, HD)
    context, row_lse = lax.map(
        lambda seq_block: attend_forward(seq_block, allowed, scaling), joined_seq
    )
    context_rows = context.reshape(seq_count * SEQ, head_width)
    middle = inputs + lax.psum_scatter(
        jnp.dot(context_rows, w_out, preferred_element_type=jnp.float32).astype(jnp.bfloat16),
        "mp",
        scatter_dimension=0,
        tiled=True,
    ).astype(jnp.float32)
    normed_two = layer_norm(middle, ln2_gain, ln2_bias).astype(jnp.bfloat16)
    rows_two = lax.all_gather(normed_two, "mp", axis=0, tiled=True)
    up_pre = jnp.dot(rows_two, w_up, preferred_element_type=jnp.float32) + b_up
    hidden = jax.nn.gelu(up_pre, approximate=True).astype(jnp.bfloat16)
    output = (
        middle
        + (
            lax.psum_scatter(
                jnp.dot(hidden, w_down, preferred_element_type=jnp.float32).astype(jnp.bfloat16),
                "mp",
                scatter_dimension=0,
                tiled=True,
            ).astype(jnp.float32)
            + b_down
        )
    ).astype(jnp.bfloat16)
    grad_out = out_grad.astype(jnp.float32)
    bias_down = jnp.sum(grad_out, axis=0)
    rows_ffn = lax.all_gather(out_grad, "mp", axis=0, tiled=True)
    grad_hidden = jnp.einsum("nd,fd->nf", rows_ffn, w_down, preferred_element_type=jnp.float32)
    grad_down = jnp.einsum("nf,nd->fd", hidden, rows_ffn, preferred_element_type=jnp.float32)
    gelu_value, gelu_pull = jax.vjp(lambda pre_act: jax.nn.gelu(pre_act, approximate=True), up_pre)
    grad_up = gelu_pull(grad_hidden)[0].astype(jnp.bfloat16)
    bias_up = jnp.sum(grad_up, axis=0, dtype=jnp.float32)
    grad_up_weight = jnp.einsum("nd,nf->df", rows_two, grad_up, preferred_element_type=jnp.float32)
    grad_normed_two = lax.psum_scatter(
        jnp.einsum("nf,df->nd", grad_up, w_up, preferred_element_type=jnp.float32).astype(
            jnp.bfloat16
        ),
        "mp",
        scatter_dimension=0,
        tiled=True,
    ).astype(jnp.float32)
    norm_value_two, norm_pull_two = jax.vjp(layer_norm, middle, ln2_gain, ln2_bias)
    grad_mid_norm, gain_two, bias_two = norm_pull_two(grad_normed_two)
    grad_middle = grad_out + grad_mid_norm
    grad_attn = grad_middle.astype(jnp.bfloat16)
    rows_attn = lax.all_gather(grad_attn, "mp", axis=0, tiled=True)
    grad_context = jnp.einsum(
        "nd,ed->ne", rows_attn, w_out, preferred_element_type=jnp.float32
    ).astype(jnp.bfloat16)
    grad_out_weight = jnp.einsum(
        "ne,nd->ed", context_rows, rows_attn, preferred_element_type=jnp.float32
    )
    grad_joined = lax.map(
        lambda seq_items: attend_backward(seq_items, allowed, scaling),
        (joined_seq, grad_context.reshape(seq_count, SEQ, local_heads, HD), row_lse),
    )
    grad_joined = grad_joined.reshape(seq_count * SEQ, 3 * head_width)
    grad_joined_weight = jnp.einsum(
        "nd,ne->de", rows_one, grad_joined, preferred_element_type=jnp.float32
    )
    grad_normed_one = lax.psum_scatter(
        jnp.einsum("ne,de->nd", grad_joined, w_joined, preferred_element_type=jnp.float32).astype(
            jnp.bfloat16
        ),
        "mp",
        scatter_dimension=0,
        tiled=True,
    ).astype(jnp.float32)
    norm_value_one, norm_pull_one = jax.vjp(layer_norm, inputs, ln1_gain, ln1_bias)
    grad_in_norm, gain_one, bias_one = norm_pull_one(grad_normed_one)
    input_grad = grad_middle + grad_in_norm
    grad_joined_weight, grad_out_weight, grad_up_weight, bias_up, grad_down = (
        lax.psum(grad_joined_weight.astype(jnp.bfloat16), "dp").astype(jnp.float32),
        lax.psum(grad_out_weight.astype(jnp.bfloat16), "dp").astype(jnp.float32),
        lax.psum(grad_up_weight.astype(jnp.bfloat16), "dp").astype(jnp.float32),
        lax.psum(bias_up.astype(jnp.bfloat16), "dp").astype(jnp.float32),
        lax.psum(grad_down.astype(jnp.bfloat16), "dp").astype(jnp.float32),
    )
    gain_one, bias_one, gain_two, bias_two, bias_down = lax.psum(
        (gain_one, bias_one, gain_two, bias_two, bias_down), ("dp", "mp")
    )
    grad_query = grad_joined_weight[:, :head_width]
    grad_key = grad_joined_weight[:, head_width : 2 * head_width]
    grad_value = grad_joined_weight[:, 2 * head_width :]
    return (
        output,
        input_grad,
        gain_one,
        bias_one,
        grad_query,
        grad_key,
        grad_value,
        grad_out_weight,
        gain_two,
        bias_two,
        grad_up_weight,
        bias_up,
        grad_down,
        bias_down,
    )


def solution(mesh):
    in_specs = (
        P(("dp", "mp"), None),
        P(("dp", "mp"), None),
        P(),
        P(),
        P(None, "mp"),
        P(None, "mp"),
        P(None, "mp"),
        P("mp", None),
        P(),
        P(),
        P(None, "mp"),
        P("mp"),
        P("mp", None),
        P(),
        P("mp", None, None),
    )
    out_specs = (
        P(("dp", "mp"), None),
        P(("dp", "mp"), None),
        P(),
        P(),
        P(None, "mp"),
        P(None, "mp"),
        P(None, "mp"),
        P("mp", None),
        P(),
        P(),
        P(None, "mp"),
        P("mp"),
        P("mp", None),
        P(),
    )
    return jax.shard_map(
        per_device, mesh=mesh, in_specs=in_specs, out_specs=out_specs, check_vma=False
    )
```

profile of v0, /device:TPU:0, one launch (start us, length us, event | category | flops | bytes accessed | tf_op | source)
XLA Modules:
  0.0 1241.2 jit_solution(840713669255894146)
XLA Ops:
  22.0 52.6 %all-gather.5.cloned.1.call-done = bf16[2048,1024]{1,0:T(8,128)(2,1)} async-done(((bf16[1024,1024]{1,0:T(8,128)(2,1)}), bf16[2048,1024]{1,0:T(8,128)(2,1)}) %all-gather.5.cloned.1.call-update) | async-done | bytes 4194320 | tf_op jit(solution)/shard_map/all_gather | solution.py:107
  74.7 11.4 convolution_convert_fusion.2
  86.1 16.3 %reshape.244 = bf16[2,1024,3,8,64]{4,3,2,1,0:T(8,128)(2,1)} reshape(bf16[2048,1536]{1,0:T(8,128)(2,1)} %convolution_convert_fusion.2) | data formatting | bytes 12582912 | tf_op jit(solution)/shard_map/reshape | solution.py:109
  102.3 14.0 %copy.56 = bf16[2,1024,3,8,64]{1,4,3,2,0:T(8,128)(2,1)} copy(bf16[2,1024,3,8,64]{4,3,2,1,0:T(8,128)(2,1)} %reshape.244) | data formatting | bytes 12582912
  116.4 113.5 %while.24 = (s32[]{:T(128)}, bf16[2,1024,8,64]{1,3,2,0:T(8,128)(2,1)}, f32[2,8,1024]{2,1,0:T(8,128)S(1)}, bf16[2,1024,3,8,64]{1,4,3,2,0:T(8,128)(2,1)}, pred[8,1024,16]{1,2,0:T(8,128)(4,1)S(1)}, /*index=5*/s32[]{:T(128)}) while((s32[]{:T(128)}, bf16[2,1024,8,64]{1,3,2,0:T(8,128)(2,1)}, f32[2,8,1024]{2,1,0:T(8,128)S(1)}, ...), condition=%wide.region_6.7_spmd.clone, body=%wide.region_3.6_spmd.clone.sunk | while | flops 2248663040 | bytes 279576704 | solution.py:110
  118.7 13.2 %fusion.101 = (f32[8,1024]{1,0:T(8,128)S(1)}, f32[8,1024,1024]{1,2,0:T(8,128)}) fusion(pred[8,1024,16]{1,2,0:T(8,128)(4,1)S(1)} %get-tuple-element.292, bf16[1024,3,8,64]{0,3,2,1:T(8,128)(2,1)S(1)} %dynamic-slice_bitcast_fusion.6), kind=kOutput, calls=%fused_computation.5.clone.1 | convolution fusion | flops 1098899456 | bytes 35815424 | tf_op jit(solution)/shard_map/while/body/eval_jaxpr/qhd,khd->hqk/dot_general | solution.py:38
  131.9 14.7 %fusion.102 = f32[8,1024]{1,0:T(8,128)S(1)} fusion(f32[8,1024,1024]{1,2,0:T(8,128)} %get-tuple-element.264, f32[8,1024]{1,0:T(8,128)S(1)} %get-tuple-element.265, pred[8,1024,16]{1,2,0:T(8,128)(4,1)S(1)} %get-tuple-element.292), kind=kLoop, calls=%fused_computation.6.clone.1 | loop fusion | flops 33546240 | bytes 33751040 | tf_op jit(solution)/shard_map/while/body/eval_jaxpr/reduce_sum | solution.py:43
  152.2 10.9 divide_convert_fusion.2
  163.1 9.8 fusion.103
  175.3 13.2 %fusion.101 = (f32[8,1024]{1,0:T(8,128)S(1)}, f32[8,1024,1024]{1,2,0:T(8,128)}) fusion(pred[8,1024,16]{1,2,0:T(8,128)(4,1)S(1)} %get-tuple-element.292, bf16[1024,3,8,64]{0,3,2,1:T(8,128)(2,1)S(1)} %dynamic-slice_bitcast_fusion.6), kind=kOutput, calls=%fused_computation.5.clone.1 | convolution fusion | flops 1098899456 | bytes 35815424 | tf_op jit(solution)/shard_map/while/body/eval_jaxpr/qhd,khd->hqk/dot_general | solution.py:38
  188.4 14.7 %fusion.102 = f32[8,1024]{1,0:T(8,128)S(1)} fusion(f32[8,1024,1024]{1,2,0:T(8,128)} %get-tuple-element.264, f32[8,1024]{1,0:T(8,128)S(1)} %get-tuple-element.265, pred[8,1024,16]{1,2,0:T(8,128)(4,1)S(1)} %get-tuple-element.292), kind=kLoop, calls=%fused_computation.6.clone.1 | loop fusion | flops 33546240 | bytes 33751040 | tf_op jit(solution)/shard_map/while/body/eval_jaxpr/reduce_sum | solution.py:43
  208.7 10.9 divide_convert_fusion.2
  219.6 9.8 fusion.103
  240.1 54.4 %reduce-scatter.5.cloned.1.call-done = bf16[1024,1024]{1,0:T(8,128)(2,1)} async-done(((bf16[2048,1024]{1,0:T(8,128)(2,1)}), bf16[1024,1024]{1,0:T(8,128)(2,1)}) %reduce-scatter.5.cloned.1.call-update) | async-done | bytes 2097168 | tf_op jit(solution)/shard_map/reduce_scatter | solution.py:114
  300.9 56.3 %all-gather.7.cloned.1.call-done = bf16[2048,1024]{1,0:T(8,128)(2,1)} async-done(((bf16[1024,1024]{1,0:T(8,128)(2,1)}), bf16[2048,1024]{1,0:T(8,128)(2,1)}) %all-gather.7.cloned.1.call-update) | async-done | bytes 4194320 | tf_op jit(solution)/shard_map/all_gather | solution.py:121
  357.2 20.6 %multiply_convert_fusion.3 = (bf16[2048,2048]{1,0:T(8,128)(2,1)}, f32[2048,2048]{1,0:T(8,128)}) fusion(f32[2048]{0:T(1024)S(1)} %copy-done.44, bf16[2048,1024]{1,0:T(8,128)(2,1)} %all-gather.7.cloned.1.call-done, bf16[1024,2048]{1,0:T(8,128)(2,1)} %param.29), kind=kOutput, calls=%fused_computation.50 | convolution fusion | flops 8631877632 | bytes 33562624 | tf_op jit(solution)/shard_map/dot_general | solution.py:122
  377.8 37.6 %all-gather.9.cloned.1.call-done = bf16[2048,1024]{1,0:T(8,128)(2,1)} async-done(((bf16[1024,1024]{1,0:T(8,128)(2,1)}), bf16[2048,1024]{1,0:T(8,128)(2,1)}) %all-gather.9.cloned.1.call-update) | async-done | bytes 4194320 | tf_op jit(solution)/shard_map/all_gather | solution.py:138
  415.4 28.1 %fusion.55 = (bf16[2048]{0:T(1024)(128)(2,1)}, bf16[2048,2048]{1,0:T(8,128)(2,1)}) fusion(f32[2048,2048]{1,0:T(8,128)} %get-tuple-element.193, f32[2048]{0:T(1024)S(1)} %copy-done.44, bf16[2048,1024]{1,0:T(8,128)(2,1)} %all-gather.9.cloned.1.call-done, bf16[2048,1024]{1,0:T(8,128)(2,1)} %param.31), kind=kOutput, calls=%fused_computation.120 | convolution fusion | flops 8682207232 | bytes 33566720 | tf_op jit(solution)/shard_map/nd,fd->nf/dot_general | solution.py:139
  443.5 12.9 %convolution_convert_fusion.6 = bf16[2048,1024]{1,0:T(8,128)(2,1)} fusion(bf16[2048,2048]{1,0:T(8,128)(2,1)} %get-tuple-element.177, bf16[1024,2048]{1,0:T(8,128)(2,1)S(1)} %copy-done.41), kind=kOutput, calls=%fused_computation.87 | convolution fusion | flops 8592031744 | bytes 16777216 | tf_op jit(solution)/shard_map/nf,df->nd/dot_general | solution.py:146
  456.5 13.8 %convolution_convert_fusion.7 = bf16[2048,1024]{1,0:T(8,128)(2,1)} fusion(bf16[2048,2048]{1,0:T(8,128)(2,1)} %get-tuple-element.192, bf16[2048,1024]{1,0:T(8,128)(2,1)} %param.31), kind=kOutput, calls=%fused_computation.88 | convolution fusion | flops 8592031744 | bytes 16777216 | tf_op jit(solution)/shard_map/dot_general | solution.py:128
  470.4 40.5 %reduce-scatter.9.cloned.1.call-done = bf16[1024,1024]{1,0:T(8,128)(2,1)} async-done(((bf16[2048,1024]{1,0:T(8,128)(2,1)}), bf16[1024,1024]{1,0:T(8,128)(2,1)}) %reduce-scatter.9.cloned.1.call-update) | async-done | bytes 2097168 | tf_op jit(solution)/shard_map/reduce_scatter | solution.py:145
  515.3 52.0 %reduce-scatter.7.cloned.1.call-done = bf16[1024,1024]{1,0:T(8,128)(2,1)} async-done(((bf16[2048,1024]{1,0:T(8,128)(2,1)}), bf16[1024,1024]{1,0:T(8,128)(2,1)}) %reduce-scatter.7.cloned.1.call-update) | async-done | bytes 2097168 | tf_op jit(solution)/shard_map/reduce_scatter | solution.py:127
  567.4 5.5 fusion.57
  576.9 14.7 %convolution_convert_fusion.9 = bf16[2048,1024]{1,0:T(8,128)(2,1)} fusion(bf16[2048,2048]{1,0:T(8,128)(2,1)} %get-tuple-element.192, bf16[2048,1024]{1,0:T(8,128)(2,1)} %all-gather.9.cloned.1.call-done), kind=kOutput, calls=%fused_computation.90 | convolution fusion | flops 8592031744 | bytes 16777216 | tf_op jit(solution)/shard_map/nf,nd->fd/dot_general | solution.py:140
  591.6 13.1 %convolution_convert_fusion.5 = bf16[1024,2048]{1,0:T(8,128)(2,1)} fusion(bf16[2048,1024]{1,0:T(8,128)(2,1)S(1)} %copy-done.43, bf16[2048,2048]{1,0:T(8,128)(2,1)} %get-tuple-element.177), kind=kOutput, calls=%fused_computation.86 | convolution fusion | flops 8592031744 | bytes 16777216 | tf_op jit(solution)/shard_map/nd,nf->df/dot_general | solution.py:144
  604.7 29.0 %all-gather.11.cloned.1.call-done = bf16[2048,1024]{1,0:T(8,128)(2,1)} async-done(((bf16[1024,1024]{1,0:T(8,128)(2,1)}), bf16[2048,1024]{1,0:T(8,128)(2,1)}) %all-gather.11.cloned.1.call-update) | async-done | bytes 4194320 | tf_op jit(solution)/shard_map/all_gather | solution.py:157
  647.3 213.0 %while.25 = (s32[]{:T(128)}, bf16[2,1024,3,8,64]{1,4,3,2,0:T(8,128)(2,1)}, bf16[2,1024,3,8,64]{1,4,3,2,0:T(8,128)(2,1)}, f32[2,8,1024]{2,1,0:T(8,128)S(1)}, bf16...) while((s32[]{:T(128)}, ...), condition=%wide.region_16.17_spmd.clone, body=%wide.region_14.16_spmd.clone.sunk | while | flops 5481422848 | bytes 287768704 | solution.py:164
  649.7 13.1 %fusion.108 = f32[8,1024,1024]{1,2,0:T(8,128)} fusion(bf16[1024,3,8,64]{0,3,2,1:T(8,128)(2,1)S(1)} %dynamic-slice_bitcast_fusion.7), kind=kOutput, calls=%fused_computation.35.clone.1 | convolution fusion | flops 1073741824 | bytes 35651584 | tf_op jit(solution)/shard_map/while/body/eval_jaxpr/qhd,khd->hqk/dot_general | solution.py:55
  662.9 23.8 %multiply_reduce_fusion.3 = (f32[8,1024]{1,0:T(8,128)S(1)}, f32[8,1024,1024]{1,2,0:T(8,128)}) fusion(f32[8,1024,1024]{1,2,0:T(8,128)} %fusion.108, f32[8,1024]{1,0:T(8,128)S(1)} %dynamic-slice_bitcast_fusion.8, pred[8,1024,16]{1,2,0:T(8,128)(4,1)S(1)} %get-tuple-element.313, bf16[1024,3,8,64]{0,3,2,1:T(8,128)(2,1)S(1)} %dynamic-slice_bitcast_fusion.7, ...), kind=kOutput, calls=%fused_computation.17.clone.1 | convolution fusion | flops 1115676672 | bytes 69402624 | tf_op jit(solution)/shard_map/while/body/eval_jaxpr/qhd,khd->hqk/dot_general | solution.py:65
  686.7 33.3 %multiply_convert_fusion.5 = (bf16[8,1024,1024]{1,2,0:T(8,128)(2,1)}, bf16[8,1024,1024]{1,2,0:T(8,128)(2,1)}) fusion(f32[8,1024,1024]{1,2,0:T(8,128)} %get-tuple-element.272, f32[8,1024,1024]{1,2,0:T(8,128)} %fusion.108, f32[8,1024]{1,0:T(8,128)S(1)} %get-tuple-element.273, f32[8,1024]{1,0:T(8,128)S(1)} %dynamic-slice_bitcast_fusion.8, ...), kind=kLoop, calls=%fused_computation.16.clone.1 | loop fusion | flops 58720256 | bytes 100859904 | tf_op jit(solution)/shard_map/while/body/eval_jaxpr/convert_element_type | solution.py:69
  720.0 11.3 fusion.109
  731.3 9.1 fusion.111
  740.5 11.3 fusion.110
  756.1 13.1 %fusion.108 = f32[8,1024,1024]{1,2,0:T(8,128)} fusion(bf16[1024,3,8,64]{0,3,2,1:T(8,128)(2,1)S(1)} %dynamic-slice_bitcast_fusion.7), kind=kOutput, calls=%fused_computation.35.clone.1 | convolution fusion | flops 1073741824 | bytes 35651584 | tf_op jit(solution)/shard_map/while/body/eval_jaxpr/qhd,khd->hqk/dot_general | solution.py:55
  769.2 23.8 %multiply_reduce_fusion.3 = (f32[8,1024]{1,0:T(8,128)S(1)}, f32[8,1024,1024]{1,2,0:T(8,128)}) fusion(f32[8,1024,1024]{1,2,0:T(8,128)} %fusion.108, f32[8,1024]{1,0:T(8,128)S(1)} %dynamic-slice_bitcast_fusion.8, pred[8,1024,16]{1,2,0:T(8,128)(4,1)S(1)} %get-tuple-element.313, bf16[1024,3,8,64]{0,3,2,1:T(8,128)(2,1)S(1)} %dynamic-slice_bitcast_fusion.7, ...), kind=kOutput, calls=%fused_computation.17.clone.1 | convolution fusion | flops 1115676672 | bytes 69402624 | tf_op jit(solution)/shard_map/while/body/eval_jaxpr/qhd,khd->hqk/dot_general | solution.py:65
  793.1 33.3 %multiply_convert_fusion.5 = (bf16[8,1024,1024]{1,2,0:T(8,128)(2,1)}, bf16[8,1024,1024]{1,2,0:T(8,128)(2,1)}) fusion(f32[8,1024,1024]{1,2,0:T(8,128)} %get-tuple-element.272, f32[8,1024,1024]{1,2,0:T(8,128)} %fusion.108, f32[8,1024]{1,0:T(8,128)S(1)} %get-tuple-element.273, f32[8,1024]{1,0:T(8,128)S(1)} %dynamic-slice_bitcast_fusion.8, ...), kind=kLoop, calls=%fused_computation.16.clone.1 | loop fusion | flops 58720256 | bytes 100859904 | tf_op jit(solution)/shard_map/while/body/eval_jaxpr/convert_element_type | solution.py:69
  826.4 11.3 fusion.109
  837.7 9.1 fusion.111
  846.8 11.3 fusion.110
  860.4 11.9 copy.61
  875.0 7.8 convolution_convert_fusion.11
  882.8 8.2 convolution_convert_fusion.3
  891.1 11.9 convolution_convert_fusion.4
  903.7 35.2 %psum.77 = bf16[2048]{0:T(1024)(128)(2,1)S(1)} all-reduce(bf16[2048]{0:T(1024)(128)(2,1)S(1)} %copy-done.38), channel_id=1, replica_groups=mesh['dp'=16,'mp'=2] {'dp'}, use_global_device_ids=true, to_apply=%region_32.33 | all-reduce | flops 2048 | bytes 8192 | tf_op jit(solution)/shard_map/psum | solution.py:187
  939.5 186.7 %all-reduce.4.cloned.1.call-done = (bf16[1024,1536]{1,0:T(8,128)(2,1)}, bf16[512,1024]{1,0:T(8,128)(2,1)}, bf16[1024,2048]{1,0:T(8,128)(2,1)}, bf16[2048,1024]{1,0:T(8,128)(2,1)}) async-done(((bf16[1024,1536]{1,0:T(8,128)(2,1)}, bf16[512,1024]{1,0:T(8,128)(2,1)}, bf16[1024,2048]{1,0:T(8,128)(2,1)}, bf16[2048,1024]{1,0:T(8,128)(2,1)}), (bf16[1024,1536]{1,0:T(8,128)(2,1)}, bf16[512,1024]{1,0:T(8,128)(2,1)}, ...) | async-done | bytes 12582928 | tf_op jit(solution)/shard_map/psum | solution.py:184
  1129.0 6.9 convert_element_type.139
  1143.3 40.2 %reduce-scatter.11.cloned.1.call-done = bf16[1024,1024]{1,0:T(8,128)(2,1)} async-done(((bf16[2048,1024]{1,0:T(8,128)(2,1)}), bf16[1024,1024]{1,0:T(8,128)(2,1)}) %reduce-scatter.11.cloned.1.call-update) | async-done | bytes 2097168 | tf_op jit(solution)/shard_map/reduce_scatter | solution.py:172
  1194.4 39.8 %all-reduce = (f32[1024]{0:T(1024)}, f32[1024]{0:T(1024)}, f32[1024]{0:T(1024)}, f32[1024]{0:T(1024)}, f32[1024]{0:T(1024)}) all-reduce(f32[1024]{0:T(1024)S(1)} %get-tuple-element.140, f32[1024]{0:T(1024)S(1)} %get-tuple-element.143, f32[1024]{0:T(1024)S(1)} %copy-done.34, ...), channel_id=1, replica_groups=mesh['dp'=16,'mp'=2] {'dp','mp'}, use_global_device_ids=true, to_apply=%region_21.22 | all-reduce | flops 5120 | bytes 40960 | tf_op jit(solution)/shard_map/psum | solution.py:190
  (166 shorter events, 102.7 us)
Async XLA Ops:
  7.2 228.5 %copy-start = (bf16[512,1024]{1,0:T(8,128)(2,1)S(1)}, bf16[512,1024]{1,0:T(8,128)(2,1)}, u32[]{:S(2)}) copy-start(bf16[512,1024]{1,0:T(8,128)(2,1)} %param.26) | copy-start | bytes 3145732
  7.2 5.7 copy-start.4
  7.2 5.7 copy-start.27
  7.2 5.7 copy-start.39
  7.2 67.4 %all-gather.5.cloned.1.call-start = ((), (), s32[]{:S(2)}) async-start(), calls=%async_computation.4 | async-start | bytes 6291456 | tf_op jit(solution)/shard_map/all_gather | solution.py:107
  9.4 2.9 copy-start.23
  9.4 5.7 copy-start.36
  15.0 3.5 copy-start.20
  15.1 279.5 %reduce-scatter.5.cloned.1.call-start = ((), (), s32[]{:S(2)}) async-start(), calls=%async_computation.5 | async-start | bytes 6291456 | tf_op jit(solution)/shard_map/reduce_scatter | solution.py:114
  131.9 20.3 %copy-start.2 = (f32[8,1024,1024]{1,2,0:T(8,128)S(1)}, f32[8,1024,1024]{1,2,0:T(8,128)}, u32[]{:S(2)}) copy-start(f32[8,1024,1024]{1,2,0:T(8,128)} %get-tuple-element.264) | copy-start | bytes 100663296 | tf_op jit(solution)/shard_map/while
  188.4 20.3 %copy-start.2 = (f32[8,1024,1024]{1,2,0:T(8,128)S(1)}, f32[8,1024,1024]{1,2,0:T(8,128)}, u32[]{:S(2)}) copy-start(f32[8,1024,1024]{1,2,0:T(8,128)} %get-tuple-element.264) | copy-start | bytes 100663296 | tf_op jit(solution)/shard_map/while
  229.8 4.4 copy-start.7
  229.8 4.4 copy-start.21
  240.0 54.5 %copy-start.5 = (bf16[1024,1024]{1,0:T(8,128)(2,1)S(1)}, bf16[1024,1024]{1,0:T(8,128)(2,1)}, u32[]{:S(2)}) copy-start(bf16[1024,1024]{1,0:T(8,128)(2,1)} %param.19) | copy-start | bytes 6291460
  240.1 57.8 %copy-start.33 = (f32[1024]{0:T(1024)S(1)}, f32[1024]{0:T(1024)}, u32[]{:S(2)}) copy-start(f32[1024]{0:T(1024)} %param.27) | copy-start | bytes 12292
  240.1 57.8 %copy-start.37 = (f32[1024]{0:T(1024)S(1)}, f32[1024]{0:T(1024)}, u32[]{:S(2)}) copy-start(f32[1024]{0:T(1024)} %param.28) | copy-start | bytes 12292
  240.1 117.1 %all-gather.7.cloned.1.call-start = ((), (), s32[]{:S(2)}) async-start(), calls=%async_computation.6 | async-start | bytes 6291456 | tf_op jit(solution)/shard_map/all_gather | solution.py:121
  297.8 59.3 %copy-start.44 = (f32[2048]{0:T(1024)S(1)}, f32[2048]{0:T(1024)}, u32[]{:S(2)}) copy-start(f32[2048]{0:T(1024)} %param.30) | copy-start | bytes 24580
  300.2 115.2 %all-gather.9.cloned.1.call-start = ((), (), s32[]{:S(2)}) async-start(), calls=%async_computation.8 | async-start | bytes 6291456 | tf_op jit(solution)/shard_map/all_gather | solution.py:138
  300.8 210.1 %reduce-scatter.9.cloned.1.call-start = ((), (), s32[]{:S(2)}) async-start(), calls=%async_computation.9 | async-start | bytes 6291456 | tf_op jit(solution)/shard_map/reduce_scatter | solution.py:145
  415.4 28.1 %copy-start.41 = (bf16[1024,2048]{1,0:T(8,128)(2,1)S(1)}, bf16[1024,2048]{1,0:T(8,128)(2,1)}, u32[]{:S(2)}) copy-start(bf16[1024,2048]{1,0:T(8,128)(2,1)} %param.29) | copy-start | bytes 12582916
  456.4 110.9 %reduce-scatter.7.cloned.1.call-start = ((), (), s32[]{:S(2)}) async-start(), calls=%async_computation.7 | async-start | bytes 6291456 | tf_op jit(solution)/shard_map/reduce_scatter | solution.py:127
  470.3 97.0 %copy-start.40 = (f32[1024]{0:T(1024)S(1)}, f32[1024]{0:T(1024)}, u32[]{:S(2)}) copy-start(f32[1024]{0:T(1024)} %param.32) | copy-start | bytes 12292
  470.3 163.4 %all-gather.11.cloned.1.call-start = ((), (), s32[]{:S(2)}) async-start(), calls=%async_computation.10 | async-start | bytes 6291456 | tf_op jit(solution)/shard_map/all_gather | solution.py:157
  567.4 7.5 copy-start.13
  576.8 549.4 %all-reduce.4.cloned.1.call-start = ((), (), s32[]{:S(2)}) async-start(), calls=%async_computation.12 | async-start | bytes 25165824 | tf_op jit(solution)/shard_map/psum | solution.py:184
  576.9 14.7 %copy-start.43 = (bf16[2048,1024]{1,0:T(8,128)(2,1)S(1)}, bf16[2048,1024]{1,0:T(8,128)(2,1)}, u32[]{:S(2)}) copy-start(bf16[2048,1024]{1,0:T(8,128)(2,1)} %all-gather.7.cloned.1.call-done) | copy-start | bytes 12582916
  641.9 5.5 copy-start.8
  641.9 5.5 copy-start.22
  649.7 13.1 %copy-start.3 = (bf16[1024,3,8,64]{0,3,2,1:T(8,128)(2,1)}, bf16[1024,3,8,64]{0,3,2,1:T(8,128)(2,1)S(1)}, u32[]{:S(2)}) copy-start(bf16[1024,3,8,64]{0,3,2,1:T(8,128)(2,1)S(1)} %dynamic-slice_bitcast_fusion.7) | copy-start | bytes 9437188 | tf_op jit(solution)/shard_map/while
  756.1 13.2 %copy-start.3 = (bf16[1024,3,8,64]{0,3,2,1:T(8,128)(2,1)}, bf16[1024,3,8,64]{0,3,2,1:T(8,128)(2,1)S(1)}, u32[]{:S(2)}) copy-start(bf16[1024,3,8,64]{0,3,2,1:T(8,128)(2,1)S(1)} %dynamic-slice_bitcast_fusion.7) | copy-start | bytes 9437188 | tf_op jit(solution)/shard_map/while
  875.0 7.8 copy-start.16
  875.0 7.8 copy-start.42
  891.1 292.4 %reduce-scatter.11.cloned.1.call-start = ((), (), s32[]{:S(2)}) async-start(), calls=%async_computation.11 | async-start | bytes 6291456 | tf_op jit(solution)/shard_map/reduce_scatter | solution.py:172
  1129.0 6.9 copy-start.17
  1135.9 4.4 copy-start.15
  1140.3 43.2 %copy-start.6 = (bf16[1024,1024]{1,0:T(8,128)(2,1)S(1)}, bf16[1024,1024]{1,0:T(8,128)(2,1)}, u32[]{:S(2)}) copy-start(bf16[1024,1024]{1,0:T(8,128)(2,1)} %param.19) | copy-start | bytes 6291460
  1140.3 43.2 %copy-start.24 = (f32[1024]{0:T(1024)S(1)}, f32[1024]{0:T(1024)}, u32[]{:S(2)}) copy-start(f32[1024]{0:T(1024)} %copy-done.23) | copy-start | bytes 12292
  1140.3 43.2 %copy-start.28 = (f32[1024]{0:T(1024)S(1)}, f32[1024]{0:T(1024)}, u32[]{:S(2)}) copy-start(f32[1024]{0:T(1024)} %param.21) | copy-start | bytes 12292
  1143.3 43.3 %copy-start.32 = (f32[1024]{0:T(1024)S(1)}, f32[1024]{0:T(1024)}, u32[]{:S(2)}) copy-start(f32[1024]{0:T(1024)} %copy-done.31) | copy-start | bytes 12292
  1143.3 43.4 %copy-start.26 = (f32[1024]{0:T(1024)S(1)}, f32[1024]{0:T(1024)}, u32[]{:S(2)}) copy-start(f32[1024]{0:T(1024)} %copy-done.25) | copy-start | bytes 12292
  1143.3 47.3 %copy-start.30 = (f32[1024]{0:T(1024)S(1)}, f32[1024]{0:T(1024)}, u32[]{:S(2)}) copy-start(f32[1024]{0:T(1024)} %copy-done.29) | copy-start | bytes 12292
  1183.5 7.1 copy-start.11
  1183.5 7.1 copy-start.12
  1183.5 7.1 copy-start.14
  1190.6 43.6 %copy-start.1 = (bf16[512,1024]{1,0:T(8,128)(2,1)S(1)}, bf16[512,1024]{1,0:T(8,128)(2,1)}, u32[]{:S(2)}) copy-start(bf16[512,1024]{1,0:T(8,128)(2,1)} %param.26) | copy-start | bytes 3145732
  1190.6 3.7 copy-start.34
  1190.7 3.7 copy-start.35
  (8 other events, 12.2 us)
Sparse Core Ops, SparseCore 0:
  15.2 59.4 all-gather.4
  240.2 54.3 reduce-scatter.4
  300.4 56.7 all-gather.6
  358.6 56.7 all-gather.8
  456.5 54.3 reduce-scatter.8
  513.0 54.2 reduce-scatter.6
  576.9 56.7 all-gather.10
  891.2 234.9 all-reduce.3
  1129.1 54.3 reduce-scatter.10
where the time goes:
time: 1250 us; the launch traced here: 1240 us
  waiting for transfers between devices  550 us (44%)
  matrix products  335 us (27%)
  other arithmetic  172 us (14%)
  local copies, waits for them, and re-layouts  93.5 us (7%)
  blocking collectives  75.1 us (6%)
  between operations  14.8 us (1%)
    psum x1, waiting for transfers between devices, per_device(): lax.psum(grad_joined_weight.astype(jnp.bfloat16), 'dp').astype(jnp.float32)  187 us
    convert_element_type x2, other arithmetic, attend_backward(): grad_scores = (attn_probs * (grad_probs - row_inner)).astype(jnp.bfloat16)  66.6 us
    all_gather x1, waiting for transfers between devices, per_device(): rows_two = lax.all_gather(normed_two, 'mp', axis=0, tiled=True)  56.3 us
    reduce_scatter x1, waiting for transfers between devices, per_device(): lax.psum_scatter(jnp.dot(context_rows, w_out, preferred_element_type=jnp....  54.4 us
    all_gather x1, waiting for transfers between devices, per_device(): rows_one = lax.all_gather(normed_one, 'mp', axis=0, tiled=True)  52.6 us
    reduce_scatter x1, waiting for transfers between devices, per_device(): lax.psum_scatter(jnp.dot(hidden, w_down, preferred_element_type=jnp.float...  52 us
    dot_general x2, matrix products, attend_backward(): jnp.einsum('qhd,khd->hqk', grad_context, value_rows, preferred_element_ty...  47.7 us
    reduce_scatter x1, waiting for transfers between devices, per_device(): lax.psum_scatter(jnp.einsum('nf,df->nd', grad_up, w_up, preferred_element...  40.5 us
  transfers between devices with their start and end apart: 9, of which 9 were waited for; matrix products, arithmetic and copies ran while one was open for 8% of the time, Pallas kernels for 0%

commit v1 on v0

--- a/solution.py
+++ b/solution.py
@@ -118,7 +118,17 @@
         tiled=True,
     ).astype(jnp.float32)
     normed_two = layer_norm(middle, ln2_gain, ln2_bias).astype(jnp.bfloat16)
-    rows_two = lax.all_gather(normed_two, "mp", axis=0, tiled=True)
+    row_out = lax.axis_index("mp")
+    view_out = lax.axis_size("mp")
+    outcome_arr, known, carry_out = (view_out, row_out, normed_two.shape[0])
+    raw_out, taken_in = (normed_two, 1)
+    while taken_in < outcome_arr:
+        n_now = lax.ppermute(
+            raw_out, "mp", [(kk, (kk - taken_in) % outcome_arr) for kk in range(outcome_arr)]
+        )
+        raw_out = jnp.concatenate([raw_out, n_now], axis=0)
+        taken_in = 2 * taken_in
+    rows_two = jnp.roll(raw_out, shift=known * carry_out, axis=0)
     up_pre = jnp.dot(rows_two, w_up, preferred_element_type=jnp.float32) + b_up
     hidden = jax.nn.gelu(up_pre, approximate=True).astype(jnp.bfloat16)
     output = (

time: 1250 us -> 1240 us (level)
    ppermute x0 -> x1, waiting for transfers between devices: none -> 82.6 us  [per_device(): lax.ppermute(raw_out, 'mp', [(kk, (kk - taken_in) % outcome_arr) for kk i...]
    all_gather x1 -> x0, waiting for transfers between devices: 56.3 us -> none  [per_device(): rows_two = lax.all_gather(normed_two, 'mp', axis=0, tiled=True)]
    all_gather x1, waiting for transfers between devices: 37.6 us -> 0.01 us  [per_device(): rows_ffn = lax.all_gather(out_grad, 'mp', axis=0, tiled=True)]
    unnamed x93 -> x97, local copies, waits for them, and re-layouts: 31.5 us -> 33.4 us
  transfers between devices with their start and end apart: 9 -> 9, of which waited for: 9 -> 8; matrix products, arithmetic and copies ran while one was open for 8% -> 9% of each run, Pallas kernels for 0% -> 0%
where the time goes in v1:
time: 1240 us; the launch traced here: 1230 us
  waiting for transfers between devices  538 us (43%)
  matrix products  331 us (27%)
  other arithmetic  179 us (14%)
  local copies, waits for them, and re-layouts  95.4 us (8%)
  blocking collectives  75.1 us (6%)
  between operations  15.1 us (1%)
    psum x1, waiting for transfers between devices, per_device(): lax.psum(grad_joined_weight.astype(jnp.bfloat16), 'dp').astype(jnp.float32)  187 us
    ppermute x1, waiting for transfers between devices, per_device(): lax.ppermute(raw_out, 'mp', [(kk, (kk - taken_in) % outcome_arr) for kk i...  82.6 us
    convert_element_type x2, other arithmetic, attend_backward(): grad_scores = (attn_probs * (grad_probs - row_inner)).astype(jnp.bfloat16)  66.6 us
    reduce_scatter x1, waiting for transfers between devices, per_device(): lax.psum_scatter(jnp.dot(context_rows, w_out, preferred_element_type=jnp....  54.4 us
    all_gather x1, waiting for transfers between devices, per_device(): rows_one = lax.all_gather(normed_one, 'mp', axis=0, tiled=True)  52.6 us
    reduce_scatter x1, waiting for transfers between devices, per_device(): lax.psum_scatter(jnp.dot(hidden, w_down, preferred_element_type=jnp.float...  52 us
    dot_general x2, matrix products, attend_backward(): jnp.einsum('qhd,khd->hqk', grad_context, value_rows, preferred_element_ty...  47.7 us
    reduce_scatter x1, waiting for transfers between devices, per_device(): lax.psum_scatter(jnp.einsum('nf,df->nd', grad_up, w_up, preferred_element...  40.5 us
  transfers between devices with their start and end apart: 9, of which 8 were waited for; matrix products, arithmetic and copies ran while one was open for 9% of the time, Pallas kernels for 0%

profile of v1, /device:TPU:0, one launch (start us, length us, event | category | flops | bytes accessed | tf_op | source)
XLA Modules:
  0.0 1234.6 jit_solution(4419521875692817850)
XLA Ops:
  22.0 52.6 %all-gather.4.cloned.1.call-done = bf16[2048,1024]{1,0:T(8,128)(2,1)} async-done(((bf16[1024,1024]{1,0:T(8,128)(2,1)}), bf16[2048,1024]{1,0:T(8,128)(2,1)}) %all-gather.4.cloned.1.call-update) | async-done | bytes 4194320 | tf_op jit(solution)/shard_map/all_gather | solution.py:107
  74.7 11.4 convolution_convert_fusion.2
  86.1 16.3 %reshape.244 = bf16[2,1024,3,8,64]{4,3,2,1,0:T(8,128)(2,1)} reshape(bf16[2048,1536]{1,0:T(8,128)(2,1)} %convolution_convert_fusion.2) | data formatting | bytes 12582912 | tf_op jit(solution)/shard_map/reshape | solution.py:109
  102.3 14.0 %copy.56 = bf16[2,1024,3,8,64]{1,4,3,2,0:T(8,128)(2,1)} copy(bf16[2,1024,3,8,64]{4,3,2,1,0:T(8,128)(2,1)} %reshape.244) | data formatting | bytes 12582912
  116.4 113.5 %while.24 = (s32[]{:T(128)}, bf16[2,1024,8,64]{1,3,2,0:T(8,128)(2,1)}, f32[2,8,1024]{2,1,0:T(8,128)S(1)}, bf16[2,1024,3,8,64]{1,4,3,2,0:T(8,128)(2,1)}, pred[8,1024,16]{1,2,0:T(8,128)(4,1)S(1)}, /*index=5*/s32[]{:T(128)}) while((s32[]{:T(128)}, bf16[2,1024,8,64]{1,3,2,0:T(8,128)(2,1)}, f32[2,8,1024]{2,1,0:T(8,128)S(1)}, ...), condition=%wide.region_6.7_spmd.clone, body=%wide.region_3.6_spmd.clone.sunk | while | flops 2248663040 | bytes 279576704 | solution.py:110
  118.7 13.2 %fusion.104 = (f32[8,1024]{1,0:T(8,128)S(1)}, f32[8,1024,1024]{1,2,0:T(8,128)}) fusion(pred[8,1024,16]{1,2,0:T(8,128)(4,1)S(1)} %get-tuple-element.292, bf16[1024,3,8,64]{0,3,2,1:T(8,128)(2,1)S(1)} %dynamic-slice_bitcast_fusion.6), kind=kOutput, calls=%fused_computation.5.clone.1 | convolution fusion | flops 1098899456 | bytes 35815424 | tf_op jit(solution)/shard_map/while/body/eval_jaxpr/qhd,khd->hqk/dot_general | solution.py:38
  131.9 14.7 %fusion.105 = f32[8,1024]{1,0:T(8,128)S(1)} fusion(f32[8,1024,1024]{1,2,0:T(8,128)} %get-tuple-element.264, f32[8,1024]{1,0:T(8,128)S(1)} %get-tuple-element.265, pred[8,1024,16]{1,2,0:T(8,128)(4,1)S(1)} %get-tuple-element.292), kind=kLoop, calls=%fused_computation.6.clone.1 | loop fusion | flops 33546240 | bytes 33751040 | tf_op jit(solution)/shard_map/while/body/eval_jaxpr/reduce_sum | solution.py:43
  152.2 10.9 divide_convert_fusion.2
  163.1 9.8 fusion.106
  175.3 13.2 %fusion.104 = (f32[8,1024]{1,0:T(8,128)S(1)}, f32[8,1024,1024]{1,2,0:T(8,128)}) fusion(pred[8,1024,16]{1,2,0:T(8,128)(4,1)S(1)} %get-tuple-element.292, bf16[1024,3,8,64]{0,3,2,1:T(8,128)(2,1)S(1)} %dynamic-slice_bitcast_fusion.6), kind=kOutput, calls=%fused_computation.5.clone.1 | convolution fusion | flops 1098899456 | bytes 35815424 | tf_op jit(solution)/shard_map/while/body/eval_jaxpr/qhd,khd->hqk/dot_general | solution.py:38
  188.4 14.7 %fusion.105 = f32[8,1024]{1,0:T(8,128)S(1)} fusion(f32[8,1024,1024]{1,2,0:T(8,128)} %get-tuple-element.264, f32[8,1024]{1,0:T(8,128)S(1)} %get-tuple-element.265, pred[8,1024,16]{1,2,0:T(8,128)(4,1)S(1)} %get-tuple-element.292), kind=kLoop, calls=%fused_computation.6.clone.1 | loop fusion | flops 33546240 | bytes 33751040 | tf_op jit(solution)/shard_map/while/body/eval_jaxpr/reduce_sum | solution.py:43
  208.7 10.9 divide_convert_fusion.2
  219.6 9.8 fusion.106
  240.1 54.4 %reduce-scatter.5.cloned.1.call-done = bf16[1024,1024]{1,0:T(8,128)(2,1)} async-done(((bf16[2048,1024]{1,0:T(8,128)(2,1)}), bf16[1024,1024]{1,0:T(8,128)(2,1)}) %reduce-scatter.5.cloned.1.call-update) | async-done | bytes 2097168 | tf_op jit(solution)/shard_map/reduce_scatter | solution.py:114
  300.6 82.6 %collective-permute-done = bf16[1024,1024]{1,0:T(8,128)(2,1)} collective-permute-done((bf16[1024,1024]{1,0:T(8,128)(2,1)}, bf16[1024,1024]{1,0:T(8,128)(2,1)}, u32[]{:S(2)}, u32[]{:S(2)}) %collective-permute-start) | collective-permute-done | bytes 2097184 | tf_op jit(solution)/shard_map/ppermute | solution.py:126
  383.3 6.9 fusion.46
  392.2 16.4 %multiply_convert_fusion.3 = (bf16[2048,2048]{1,0:T(8,128)(2,1)}, f32[2048,2048]{1,0:T(8,128)}) fusion(f32[2048]{0:T(1024)S(1)} %copy-done.46, bf16[2048,1024]{1,0:T(8,128)(2,1)S(1)} %fusion.46, bf16[1024,2048]{1,0:T(8,128)(2,1)S(1)} %copy-done.43), kind=kOutput, calls=%fused_computation.50 | convolution fusion | flops 8631877632 | bytes 33562624 | tf_op jit(solution)/shard_map/dot_general | solution.py:132
  408.6 28.0 %fusion.58 = (bf16[2048]{0:T(1024)(128)(2,1)}, bf16[2048,2048]{1,0:T(8,128)(2,1)}) fusion(f32[2048,2048]{1,0:T(8,128)} %get-tuple-element.193, f32[2048]{0:T(1024)S(1)} %copy-done.46, bf16[2048,1024]{1,0:T(8,128)(2,1)} %all-gather.6.cloned.1.call-done, bf16[2048,1024]{1,0:T(8,128)(2,1)} %param.31), kind=kOutput, calls=%fused_computation.127 | convolution fusion | flops 8682207232 | bytes 33566720 | tf_op jit(solution)/shard_map/nd,fd->nf/dot_general | solution.py:149
  436.6 12.9 %convolution_convert_fusion.6 = bf16[2048,1024]{1,0:T(8,128)(2,1)} fusion(bf16[2048,2048]{1,0:T(8,128)(2,1)} %get-tuple-element.177, bf16[1024,2048]{1,0:T(8,128)(2,1)S(1)} %copy-done.44), kind=kOutput, calls=%fused_computation.94 | convolution fusion | flops 8592031744 | bytes 16777216 | tf_op jit(solution)/shard_map/nf,df->nd/dot_general | solution.py:156
  449.6 13.8 %convolution_convert_fusion.7 = bf16[2048,1024]{1,0:T(8,128)(2,1)} fusion(bf16[2048,2048]{1,0:T(8,128)(2,1)} %get-tuple-element.192, bf16[2048,1024]{1,0:T(8,128)(2,1)} %param.31), kind=kOutput, calls=%fused_computation.95 | convolution fusion | flops 8592031744 | bytes 16777216 | tf_op jit(solution)/shard_map/dot_general | solution.py:138
  463.5 40.5 %reduce-scatter.9.cloned.1.call-done = bf16[1024,1024]{1,0:T(8,128)(2,1)} async-done(((bf16[2048,1024]{1,0:T(8,128)(2,1)}), bf16[1024,1024]{1,0:T(8,128)(2,1)}) %reduce-scatter.9.cloned.1.call-update) | async-done | bytes 2097168 | tf_op jit(solution)/shard_map/reduce_scatter | solution.py:155
  508.5 52.0 %reduce-scatter.7.cloned.1.call-done = bf16[1024,1024]{1,0:T(8,128)(2,1)} async-done(((bf16[2048,1024]{1,0:T(8,128)(2,1)}), bf16[1024,1024]{1,0:T(8,128)(2,1)}) %reduce-scatter.7.cloned.1.call-update) | async-done | bytes 2097168 | tf_op jit(solution)/shard_map/reduce_scatter | solution.py:137
  560.5 5.5 fusion.60
  570.0 14.7 %convolution_convert_fusion.9 = bf16[2048,1024]{1,0:T(8,128)(2,1)} fusion(bf16[2048,2048]{1,0:T(8,128)(2,1)} %get-tuple-element.192, bf16[2048,1024]{1,0:T(8,128)(2,1)} %all-gather.6.cloned.1.call-done), kind=kOutput, calls=%fused_computation.97 | convolution fusion | flops 8592031744 | bytes 16777216 | tf_op jit(solution)/shard_map/nf,nd->fd/dot_general | solution.py:150
  584.7 13.1 %convolution_convert_fusion.5 = bf16[1024,2048]{1,0:T(8,128)(2,1)} fusion(bf16[2048,1024]{1,0:T(8,128)(2,1)S(1)} %copy-done.19, bf16[2048,2048]{1,0:T(8,128)(2,1)} %get-tuple-element.177), kind=kOutput, calls=%fused_computation.93 | convolution fusion | flops 8592031744 | bytes 16777216 | tf_op jit(solution)/shard_map/nd,nf->df/dot_general | solution.py:154
  597.8 29.0 %all-gather.8.cloned.1.call-done = bf16[2048,1024]{1,0:T(8,128)(2,1)} async-done(((bf16[1024,1024]{1,0:T(8,128)(2,1)}), bf16[2048,1024]{1,0:T(8,128)(2,1)}) %all-gather.8.cloned.1.call-update) | async-done | bytes 4194320 | tf_op jit(solution)/shard_map/all_gather | solution.py:167
  640.5 213.0 %while.25 = (s32[]{:T(128)}, bf16[2,1024,3,8,64]{1,4,3,2,0:T(8,128)(2,1)}, bf16[2,1024,3,8,64]{1,4,3,2,0:T(8,128)(2,1)}, f32[2,8,1024]{2,1,0:T(8,128)S(1)}, bf16...) while((s32[]{:T(128)}, ...), condition=%wide.region_16.17_spmd.clone, body=%wide.region_14.16_spmd.clone.sunk | while | flops 5481422848 | bytes 287768704 | solution.py:174
  642.9 13.1 %fusion.111 = f32[8,1024,1024]{1,2,0:T(8,128)} fusion(bf16[1024,3,8,64]{0,3,2,1:T(8,128)(2,1)S(1)} %dynamic-slice_bitcast_fusion.7), kind=kOutput, calls=%fused_computation.35.clone.1 | convolution fusion | flops 1073741824 | bytes 35651584 | tf_op jit(solution)/shard_map/while/body/eval_jaxpr/qhd,khd->hqk/dot_general | solution.py:55
  656.0 23.8 %multiply_reduce_fusion.3 = (f32[8,1024]{1,0:T(8,128)S(1)}, f32[8,1024,1024]{1,2,0:T(8,128)}) fusion(f32[8,1024,1024]{1,2,0:T(8,128)} %fusion.111, f32[8,1024]{1,0:T(8,128)S(1)} %dynamic-slice_bitcast_fusion.8, pred[8,1024,16]{1,2,0:T(8,128)(4,1)S(1)} %get-tuple-element.313, bf16[1024,3,8,64]{0,3,2,1:T(8,128)(2,1)S(1)} %dynamic-slice_bitcast_fusion.7, ...), kind=kOutput, calls=%fused_computation.17.clone.1 | convolution fusion | flops 1115676672 | bytes 69402624 | tf_op jit(solution)/shard_map/while/body/eval_jaxpr/qhd,khd->hqk/dot_general | solution.py:65
  679.9 33.3 %multiply_convert_fusion.5 = (bf16[8,1024,1024]{1,2,0:T(8,128)(2,1)}, bf16[8,1024,1024]{1,2,0:T(8,128)(2,1)}) fusion(f32[8,1024,1024]{1,2,0:T(8,128)} %get-tuple-element.272, f32[8,1024,1024]{1,2,0:T(8,128)} %fusion.111, f32[8,1024]{1,0:T(8,128)S(1)} %get-tuple-element.273, f32[8,1024]{1,0:T(8,128)S(1)} %dynamic-slice_bitcast_fusion.8, ...), kind=kLoop, calls=%fused_computation.16.clone.1 | loop fusion | flops 58720256 | bytes 100859904 | tf_op jit(solution)/shard_map/while/body/eval_jaxpr/convert_element_type | solution.py:69
  713.2 11.3 fusion.112
  724.5 9.1 fusion.114
  733.6 11.3 fusion.113
  749.2 13.1 %fusion.111 = f32[8,1024,1024]{1,2,0:T(8,128)} fusion(bf16[1024,3,8,64]{0,3,2,1:T(8,128)(2,1)S(1)} %dynamic-slice_bitcast_fusion.7), kind=kOutput, calls=%fused_computation.35.clone.1 | convolution fusion | flops 1073741824 | bytes 35651584 | tf_op jit(solution)/shard_map/while/body/eval_jaxpr/qhd,khd->hqk/dot_general | solution.py:55
  762.4 23.8 %multiply_reduce_fusion.3 = (f32[8,1024]{1,0:T(8,128)S(1)}, f32[8,1024,1024]{1,2,0:T(8,128)}) fusion(f32[8,1024,1024]{1,2,0:T(8,128)} %fusion.111, f32[8,1024]{1,0:T(8,128)S(1)} %dynamic-slice_bitcast_fusion.8, pred[8,1024,16]{1,2,0:T(8,128)(4,1)S(1)} %get-tuple-element.313, bf16[1024,3,8,64]{0,3,2,1:T(8,128)(2,1)S(1)} %dynamic-slice_bitcast_fusion.7, ...), kind=kOutput, calls=%fused_computation.17.clone.1 | convolution fusion | flops 1115676672 | bytes 69402624 | tf_op jit(solution)/shard_map/while/body/eval_jaxpr/qhd,khd->hqk/dot_general | solution.py:65
  786.2 33.3 %multiply_convert_fusion.5 = (bf16[8,1024,1024]{1,2,0:T(8,128)(2,1)}, bf16[8,1024,1024]{1,2,0:T(8,128)(2,1)}) fusion(f32[8,1024,1024]{1,2,0:T(8,128)} %get-tuple-element.272, f32[8,1024,1024]{1,2,0:T(8,128)} %fusion.111, f32[8,1024]{1,0:T(8,128)S(1)} %get-tuple-element.273, f32[8,1024]{1,0:T(8,128)S(1)} %dynamic-slice_bitcast_fusion.8, ...), kind=kLoop, calls=%fused_computation.16.clone.1 | loop fusion | flops 58720256 | bytes 100859904 | tf_op jit(solution)/shard_map/while/body/eval_jaxpr/convert_element_type | solution.py:69
  819.5 11.3 fusion.112
  830.8 9.1 fusion.114
  840.0 11.3 fusion.113
  853.5 11.9 copy.61
  868.2 7.8 convolution_convert_fusion.11
  876.0 8.2 convolution_convert_fusion.3
  884.3 11.9 convolution_convert_fusion.4
  896.8 35.2 %psum.77 = bf16[2048]{0:T(1024)(128)(2,1)S(1)} all-reduce(bf16[2048]{0:T(1024)(128)(2,1)S(1)} %copy-done.40), channel_id=1, replica_groups=mesh['dp'=16,'mp'=2] {'dp'}, use_global_device_ids=true, to_apply=%region_32.33 | all-reduce | flops 2048 | bytes 8192 | tf_op jit(solution)/shard_map/psum | solution.py:197
  932.7 186.7 %all-reduce.4.cloned.1.call-done = (bf16[1024,1536]{1,0:T(8,128)(2,1)}, bf16[512,1024]{1,0:T(8,128)(2,1)}, bf16[1024,2048]{1,0:T(8,128)(2,1)}, bf16[2048,1024]{1,0:T(8,128)(2,1)}) async-done(((bf16[1024,1536]{1,0:T(8,128)(2,1)}, bf16[512,1024]{1,0:T(8,128)(2,1)}, bf16[1024,2048]{1,0:T(8,128)(2,1)}, bf16[2048,1024]{1,0:T(8,128)(2,1)}), (bf16[1024,1536]{1,0:T(8,128)(2,1)}, bf16[512,1024]{1,0:T(8,128)(2,1)}, ...) | async-done | bytes 12582928 | tf_op jit(solution)/shard_map/psum | solution.py:194
  1122.1 6.9 convert_element_type.139
  1136.5 40.2 %reduce-scatter.11.cloned.1.call-done = bf16[1024,1024]{1,0:T(8,128)(2,1)} async-done(((bf16[2048,1024]{1,0:T(8,128)(2,1)}), bf16[1024,1024]{1,0:T(8,128)(2,1)}) %reduce-scatter.11.cloned.1.call-update) | async-done | bytes 2097168 | tf_op jit(solution)/shard_map/reduce_scatter | solution.py:182
  1187.5 39.8 %all-reduce = (f32[1024]{0:T(1024)}, f32[1024]{0:T(1024)}, f32[1024]{0:T(1024)}, f32[1024]{0:T(1024)}, f32[1024]{0:T(1024)}) all-reduce(f32[1024]{0:T(1024)S(1)} %get-tuple-element.140, f32[1024]{0:T(1024)S(1)} %get-tuple-element.143, f32[1024]{0:T(1024)S(1)} %copy-done.36, ...), channel_id=1, replica_groups=mesh['dp'=16,'mp'=2] {'dp','mp'}, use_global_device_ids=true, to_apply=%region_21.22 | all-reduce | flops 5120 | bytes 40960 | tf_op jit(solution)/shard_map/psum | solution.py:200
  (170 shorter events, 104.4 us)
Async XLA Ops:
  7.2 228.5 %copy-start = (bf16[512,1024]{1,0:T(8,128)(2,1)S(1)}, bf16[512,1024]{1,0:T(8,128)(2,1)}, u32[]{:S(2)}) copy-start(bf16[512,1024]{1,0:T(8,128)(2,1)} %param.26) | copy-start | bytes 3145732
  7.2 5.7 copy-start.4
  7.2 5.7 copy-start.29
  7.2 5.7 copy-start.41
  7.2 67.4 %all-gather.4.cloned.1.call-start = ((), (), s32[]{:S(2)}) async-start(), calls=%async_computation.4 | async-start | bytes 6291456 | tf_op jit(solution)/shard_map/all_gather | solution.py:107
  9.4 5.7 copy-start.38
  15.0 3.5 copy-start.22
  15.1 279.5 %reduce-scatter.5.cloned.1.call-start = ((), (), s32[]{:S(2)}) async-start(), calls=%async_computation.5 | async-start | bytes 6291456 | tf_op jit(solution)/shard_map/reduce_scatter | solution.py:114
  131.9 20.3 %copy-start.2 = (f32[8,1024,1024]{1,2,0:T(8,128)S(1)}, f32[8,1024,1024]{1,2,0:T(8,128)}, u32[]{:S(2)}) copy-start(f32[8,1024,1024]{1,2,0:T(8,128)} %get-tuple-element.264) | copy-start | bytes 100663296 | tf_op jit(solution)/shard_map/while
  188.4 20.3 %copy-start.2 = (f32[8,1024,1024]{1,2,0:T(8,128)S(1)}, f32[8,1024,1024]{1,2,0:T(8,128)}, u32[]{:S(2)}) copy-start(f32[8,1024,1024]{1,2,0:T(8,128)} %get-tuple-element.264) | copy-start | bytes 100663296 | tf_op jit(solution)/shard_map/while
  229.8 4.4 copy-start.7
  229.8 4.4 copy-start.23
  240.0 54.5 %copy-start.5 = (bf16[1024,1024]{1,0:T(8,128)(2,1)S(1)}, bf16[1024,1024]{1,0:T(8,128)(2,1)}, u32[]{:S(2)}) copy-start(bf16[1024,1024]{1,0:T(8,128)(2,1)} %param.19) | copy-start | bytes 6291460
  240.1 57.8 %copy-start.35 = (f32[1024]{0:T(1024)S(1)}, f32[1024]{0:T(1024)}, u32[]{:S(2)}) copy-start(f32[1024]{0:T(1024)} %param.27) | copy-start | bytes 12292
  240.1 57.8 %copy-start.39 = (f32[1024]{0:T(1024)S(1)}, f32[1024]{0:T(1024)}, u32[]{:S(2)}) copy-start(f32[1024]{0:T(1024)} %param.28) | copy-start | bytes 12292
  240.1 168.5 %all-gather.6.cloned.1.call-start = ((), (), s32[]{:S(2)}) async-start(), calls=%async_computation.7 | async-start | bytes 6291456 | tf_op jit(solution)/shard_map/all_gather | solution.py:148
  300.2 83.1 %collective-permute-start = (bf16[1024,1024]{1,0:T(8,128)(2,1)}, bf16[1024,1024]{1,0:T(8,128)(2,1)}, u32[]{:S(2)}, u32[]{:S(2)}) collective-permute-start(bf16[1024,1024]{1,0:T(8,128)(2,1)} %add_convert_fusion.1), channel_id=1, source_target_pairs={{0,1},{1,0},{2,3},{3,2},{4,5},{5,4},{6,7},{7,6},{8,9},{9,8},{10,11... | collective-permute-start | bytes 6291464 | tf_op jit(solution)/shard_map/ppermute | solution.py:126
  300.6 203.5 %reduce-scatter.9.cloned.1.call-start = ((), (), s32[]{:S(2)}) async-start(), calls=%async_computation.8 | async-start | bytes 6291456 | tf_op jit(solution)/shard_map/reduce_scatter | solution.py:155
  300.6 91.5 %copy-start.43 = (bf16[1024,2048]{1,0:T(8,128)(2,1)S(1)}, bf16[1024,2048]{1,0:T(8,128)(2,1)}, u32[]{:S(2)}) copy-start(bf16[1024,2048]{1,0:T(8,128)(2,1)} %param.29) | copy-start | bytes 12582916
  300.6 91.5 %copy-start.46 = (f32[2048]{0:T(1024)S(1)}, f32[2048]{0:T(1024)}, u32[]{:S(2)}) copy-start(f32[2048]{0:T(1024)} %param.30) | copy-start | bytes 24580
  408.6 28.0 %copy-start.44 = (bf16[1024,2048]{1,0:T(8,128)(2,1)S(1)}, bf16[1024,2048]{1,0:T(8,128)(2,1)}, u32[]{:S(2)}) copy-start(bf16[1024,2048]{1,0:T(8,128)(2,1)} %param.29) | copy-start | bytes 12582916
  449.6 110.9 %reduce-scatter.7.cloned.1.call-start = ((), (), s32[]{:S(2)}) async-start(), calls=%async_computation.6 | async-start | bytes 6291456 | tf_op jit(solution)/shard_map/reduce_scatter | solution.py:137
  463.5 97.0 %copy-start.42 = (f32[1024]{0:T(1024)S(1)}, f32[1024]{0:T(1024)}, u32[]{:S(2)}) copy-start(f32[1024]{0:T(1024)} %param.32) | copy-start | bytes 12292
  463.5 163.4 %all-gather.8.cloned.1.call-start = ((), (), s32[]{:S(2)}) async-start(), calls=%async_computation.9 | async-start | bytes 6291456 | tf_op jit(solution)/shard_map/all_gather | solution.py:167
  560.5 7.5 copy-start.13
  569.9 549.4 %all-reduce.4.cloned.1.call-start = ((), (), s32[]{:S(2)}) async-start(), calls=%async_computation.11 | async-start | bytes 25165824 | tf_op jit(solution)/shard_map/psum | solution.py:194
  570.0 14.7 %copy-start.19 = (bf16[2048,1024]{1,0:T(8,128)(2,1)S(1)}, bf16[2048,1024]{1,0:T(8,128)(2,1)}, u32[]{:S(2)}) copy-start(bf16[2048,1024]{1,0:T(8,128)(2,1)} %copy-done.18) | copy-start | bytes 12582916
  635.0 5.5 copy-start.8
  635.0 5.5 copy-start.24
  642.9 13.2 %copy-start.3 = (bf16[1024,3,8,64]{0,3,2,1:T(8,128)(2,1)}, bf16[1024,3,8,64]{0,3,2,1:T(8,128)(2,1)S(1)}, u32[]{:S(2)}) copy-start(bf16[1024,3,8,64]{0,3,2,1:T(8,128)(2,1)S(1)} %dynamic-slice_bitcast_fusion.7) | copy-start | bytes 9437188 | tf_op jit(solution)/shard_map/while
  749.2 13.2 %copy-start.3 = (bf16[1024,3,8,64]{0,3,2,1:T(8,128)(2,1)}, bf16[1024,3,8,64]{0,3,2,1:T(8,128)(2,1)S(1)}, u32[]{:S(2)}) copy-start(bf16[1024,3,8,64]{0,3,2,1:T(8,128)(2,1)S(1)} %dynamic-slice_bitcast_fusion.7) | copy-start | bytes 9437188 | tf_op jit(solution)/shard_map/while
  868.1 7.8 copy-start.16
  868.2 7.8 copy-start.45
  884.2 292.4 %reduce-scatter.11.cloned.1.call-start = ((), (), s32[]{:S(2)}) async-start(), calls=%async_computation.10 | async-start | bytes 6291456 | tf_op jit(solution)/shard_map/reduce_scatter | solution.py:182
  1122.1 6.9 copy-start.17
  1129.0 4.4 copy-start.15
  1133.4 43.2 %copy-start.6 = (bf16[1024,1024]{1,0:T(8,128)(2,1)S(1)}, bf16[1024,1024]{1,0:T(8,128)(2,1)}, u32[]{:S(2)}) copy-start(bf16[1024,1024]{1,0:T(8,128)(2,1)} %param.19) | copy-start | bytes 6291460
  1133.4 43.2 %copy-start.26 = (f32[1024]{0:T(1024)S(1)}, f32[1024]{0:T(1024)}, u32[]{:S(2)}) copy-start(f32[1024]{0:T(1024)} %copy-done.25) | copy-start | bytes 12292
  1133.4 43.2 %copy-start.30 = (f32[1024]{0:T(1024)S(1)}, f32[1024]{0:T(1024)}, u32[]{:S(2)}) copy-start(f32[1024]{0:T(1024)} %param.21) | copy-start | bytes 12292
  1136.4 43.3 %copy-start.34 = (f32[1024]{0:T(1024)S(1)}, f32[1024]{0:T(1024)}, u32[]{:S(2)}) copy-start(f32[1024]{0:T(1024)} %copy-done.33) | copy-start | bytes 12292
  1136.4 43.3 %copy-start.28 = (f32[1024]{0:T(1024)S(1)}, f32[1024]{0:T(1024)}, u32[]{:S(2)}) copy-start(f32[1024]{0:T(1024)} %copy-done.27) | copy-start | bytes 12292
  1136.5 47.3 %copy-start.32 = (f32[1024]{0:T(1024)S(1)}, f32[1024]{0:T(1024)}, u32[]{:S(2)}) copy-start(f32[1024]{0:T(1024)} %copy-done.31) | copy-start | bytes 12292
  1176.6 7.1 copy-start.11
  1176.6 7.1 copy-start.12
  1176.7 7.1 copy-start.14
  1183.7 43.6 %copy-start.1 = (bf16[512,1024]{1,0:T(8,128)(2,1)S(1)}, bf16[512,1024]{1,0:T(8,128)(2,1)}, u32[]{:S(2)}) copy-start(bf16[512,1024]{1,0:T(8,128)(2,1)} %param.26) | copy-start | bytes 3145732
  1183.8 3.7 copy-start.36
  1183.8 3.7 copy-start.37
  (10 other events, 17.0 us)
Sparse Core Ops, SparseCore 0:
  15.2 59.4 all-gather.3
  240.2 54.3 reduce-scatter.4
  300.7 92.2 all-gather.5
  449.7 54.2 reduce-scatter.8
  506.2 54.3 reduce-scatter.6
  570.1 56.7 all-gather.7
  884.3 234.9 all-reduce.3
  1122.3 54.3 reduce-scatter.10
